TPU v7x, 512 devices: a whole 4x4x16 slice. The times are simulated.
512 devices in a mesh: dp: 16 (over x, y), expert: 32 (over z, core).
Axes of the slice: x: 4, y: 4, z: 16, core: 2. Of those that a mesh axis runs over, the one named last changes fastest.
Arguments:
- tokens: bfloat16 [65536, 3584], P(('dp', 'expert')), may hold values from -6 to 6
- cotangent: bfloat16 [65536, 3584], P(('dp', 'expert')), may hold values from -6 to 6
- route_weight: float32 [65536, 8], P(('dp', 'expert')), may hold values from 0.05 to 0.5
- expert_ids: int32 [65536, 8], P(('dp', 'expert')), may hold values from 0 to 255, as said below
- live_tokens: int32 [512], P(('dp', 'expert')), may hold values from 1 to 128, 49152 in all
- replica_plan: int32 [512, 4], P(('dp', 'expert')), may hold values 0 or 1
- w_gate: bfloat16 [3584, 8192], P('dp', 'expert'), may hold values from -0.09375 to 0.09375
- w_up: bfloat16 [3584, 8192], P('dp', 'expert'), may hold values from -0.09375 to 0.09375
- w_down: bfloat16 [8192, 3584], P('expert', 'dp'), may hold values from -0.125 to 0.125
- scale_gate: float32 [28, 64], P(None, 'expert'), may hold values from 0.5 to 2
- scale_up: float32 [28, 64], P(None, 'expert'), may hold values from 0.5 to 2
- scale_down: float32 [64, 28], P('expert'), may hold values from 0.5 to 2
Outputs:
- d_tokens: bfloat16 [65536, 3584], P(('dp', 'expert'))
- grad_gate: bfloat16 [3584, 8192], P('dp', 'expert')
- grad_up: bfloat16 [3584, 8192], P('dp', 'expert')
- grad_down: bfloat16 [8192, 3584], P('expert', 'dp')
Inputs may be any that keep to these rules, and one draw needn't show every extreme that they name: `expert_ids`: the 8 ids of one token are distinct.
All inputs are finite; a program needn't handle non-finite values. No bound on the sum of `live_tokens` or of `replica_plan` on one device may be relied on, other than what follows from the above.
Results may differ from a plain program's by a relative error of at most 0.012.
Values may be sent and summed in bfloat16 or wider, within the bound.
A program may use at most 64 MiB of HBM per device.

v0:
```python
import jax
import jax.numpy as jnp
from jax import lax
from jax.sharding import PartitionSpec as P

HSH = 8
CAP = 4


def dequantize(values, scale):
    block_rows = values.shape[0] // scale.shape[0]
    block_cols = values.shape[1] // scale.shape[1]
    spread = jnp.repeat(jnp.repeat(scale, block_rows, axis=0), block_cols, axis=1)
    return (values.astype(jnp.float32) * spread).astype(jnp.bfloat16)


def route_rows(tokens, cotangent, route_weight, expert_ids, live_count, plan, experts, capacity):
    count = tokens.shape[0]
    token_index = jnp.arange(count, dtype=jnp.int32)
    expert_index = jnp.arange(experts, dtype=jnp.int32)
    matches = expert_ids[:, None, :] == expert_index[None, :, None]
    routed = jnp.any(matches, axis=2) & (token_index < live_count)[:, None]
    to_replica = (token_index % 2 == 1)[:, None] & (plan[None, :] == 1)
    in_lists = jnp.stack([routed & ~to_replica, routed & to_replica], axis=2).astype(jnp.int32)
    position = jnp.cumsum(in_lists, axis=0) - 1
    capacity_index = jnp.arange(capacity, dtype=jnp.int32)
    selected = ((in_lists[..., None] == 1) & (position[..., None] == capacity_index)).astype(
        jnp.float32
    )
    weight_sum = jnp.sum(jnp.where(matches, route_weight[:, None, :], jnp.float32(0.0)), axis=2)
    row_weight = jnp.sum(selected * weight_sum[:, :, None, None], axis=0)
    flat = selected.reshape(count, -1)
    picker = flat.T.astype(jnp.bfloat16)
    token_rows = jnp.dot(picker, tokens, preferred_element_type=jnp.float32).astype(jnp.bfloat16)
    cot_picked = jnp.dot(picker, cotangent, preferred_element_type=jnp.float32)
    cot_rows = (row_weight.reshape(-1, 1) * cot_picked).astype(jnp.bfloat16)
    shape = (experts, 2, capacity, tokens.shape[1])
    return (flat, token_rows.reshape(shape), cot_rows.reshape(shape))


def expert_terms(token_rows, cot_rows, gate_w, up_w, down_w):
    by_hidden = (((1,), (1,)), ((), ()))
    by_rows = (((0,), (0,)), ((), ()))
    gate_pre = jnp.dot(token_rows, gate_w, preferred_element_type=jnp.float32)
    up_pre = jnp.dot(token_rows, up_w, preferred_element_type=jnp.float32)
    gate_sig = jax.nn.sigmoid(gate_pre)
    swish = gate_pre * gate_sig
    d_hidden = lax.dot_general(cot_rows, down_w, by_hidden, preferred_element_type=jnp.float32)
    hidden = (swish * up_pre).astype(jnp.bfloat16)
    d_up = (d_hidden * swish).astype(jnp.bfloat16)
    d_gate = (d_hidden * up_pre * gate_sig * (1.0 + gate_pre * (1.0 - gate_sig))).astype(
        jnp.bfloat16
    )
    grad_g = lax.dot_general(
        token_rows, d_gate, by_rows, preferred_element_type=jnp.float32
    ).astype(jnp.bfloat16)
    grad_u = lax.dot_general(token_rows, d_up, by_rows, preferred_element_type=jnp.float32).astype(
        jnp.bfloat16
    )
    grad_d = lax.dot_general(cot_rows, hidden, by_rows, preferred_element_type=jnp.float32).astype(
        jnp.bfloat16
    )
    dx_part = lax.dot_general(d_gate, gate_w, by_hidden, preferred_element_type=jnp.float32)
    dx_part = dx_part + lax.dot_general(d_up, up_w, by_hidden, preferred_element_type=jnp.float32)
    return (grad_g, grad_u, grad_d, dx_part.astype(jnp.bfloat16))


def fan_out(rows, members):
    slot_count = rows.shape[0]
    spread = jnp.broadcast_to(rows[:, None], (slot_count, members // slot_count) + rows.shape[1:])
    return spread.reshape((members,) + rows.shape[1:])


def send_rows(token_rows, cot_rows, members):
    return (
        lax.all_to_all(
            fan_out(token_rows, members), "expert", split_axis=0, concat_axis=0, tiled=True
        ),
        lax.all_to_all(
            fan_out(cot_rows, members), "expert", split_axis=0, concat_axis=0, tiled=True
        ),
    )


def on_device(
    tokens,
    cotangent,
    route_weight,
    expert_ids,
    live_tokens,
    replica_plan,
    w_gate,
    w_up,
    w_down,
    scale_gate,
    scale_up,
    scale_down,
):
    members = lax.axis_size("expert")
    groups = lax.axis_size("dp")
    slot_count = members // HSH
    width = tokens.shape[1]
    flat, token_rows, cot_rows = route_rows(
        tokens,
        cotangent,
        route_weight,
        expert_ids,
        live_tokens[0],
        replica_plan[0],
        slot_count,
        CAP,
    )
    gathered = (
        lax.all_gather(w_gate, "dp", axis=0, tiled=True),
        lax.all_gather(w_up, "dp", axis=0, tiled=True),
        lax.all_gather(w_down, "dp", axis=1, tiled=True),
    )
    full_gate, full_up, full_down = gathered
    recv_tokens, recv_cots = send_rows(token_rows, cot_rows, members)
    own_gate = dequantize(full_gate, scale_gate)
    own_up = dequantize(full_up, scale_up)
    own_down = dequantize(full_down, scale_down)
    leading = expert_terms(
        recv_tokens[:, 0].reshape(-1, width),
        recv_cots[:, 0].reshape(-1, width),
        own_gate,
        own_up,
        own_down,
    )
    trailing = expert_terms(
        recv_tokens[:, 1].reshape(-1, width),
        recv_cots[:, 1].reshape(-1, width),
        own_gate,
        own_up,
        own_down,
    )
    dx_parts = jnp.stack(
        [leading[3].reshape(members, CAP, width), trailing[3].reshape(members, CAP, width)], axis=1
    )
    returned = lax.all_to_all(dx_parts, "expert", split_axis=0, concat_axis=0, tiled=True)
    summed = jnp.sum(returned.astype(jnp.float32).reshape(slot_count, HSH, 2, CAP, width), axis=1)
    sum_gate = (leading[0].astype(jnp.float32) + trailing[0].astype(jnp.float32)).astype(
        jnp.bfloat16
    )
    sum_up = (leading[1].astype(jnp.float32) + trailing[1].astype(jnp.float32)).astype(jnp.bfloat16)
    sum_down = (leading[2].astype(jnp.float32) + trailing[2].astype(jnp.float32)).astype(
        jnp.bfloat16
    )
    stacked = jnp.stack([sum_gate, sum_up, sum_down], axis=0)
    received = lax.all_to_all(stacked, "dp", split_axis=1, concat_axis=0, tiled=True)
    rows_here = received.shape[1]
    totals = jnp.sum(received.astype(jnp.float32).reshape(groups, 3, rows_here, -1), axis=0)
    totals = totals.astype(jnp.bfloat16)
    d_tokens = jnp.dot(flat, summed.reshape(-1, width), precision=lax.Precision.HIGHEST).astype(
        jnp.bfloat16
    )
    return (d_tokens, totals[0], totals[1], totals[2].T)


def solution(mesh):
    return jax.shard_map(
        on_device,
        mesh=mesh,
        in_specs=(
            P(("dp", "expert"), None),
            P(("dp", "expert"), None),
            P(("dp", "expert"), None),
            P(("dp", "expert"), None),
            P(("dp", "expert")),
            P(("dp", "expert"), None),
            P("dp", "expert"),
            P("dp", "expert"),
            P("expert", "dp"),
            P(None, "expert"),
            P(None, "expert"),
            P("expert", None),
        ),
        out_specs=(
            P(("dp", "expert"), None),
            P("dp", "expert"),
            P("dp", "expert"),
            P("expert", "dp"),
        ),
        check_vma=False,
    )
```

profile of v0, /device:TPU:20, one launch (start us, length us, event | category | flops | bytes accessed | tf_op | source)
XLA Modules:
  0.0 513.7 jit_solution(6729519328803929821)
XLA Ops:
  12.1 15.6 %all-to-all-start.1 = ((bf16[32,2,4,3584]{3,2,1,0:T(4,128)(2,1)}), bf16[32,2,4,3584]{3,2,1,0:T(4,128)(2,1)S(1)}, u32[]{:S(2)}, u32[]{:S(2)}) async-start(bf16[32,2,4,3584]{3,2,1,0:T(4,128)(2,1)} %bitcast.102), calls=%async_computation.1 | async-start | bytes 3670016 | tf_op jit(solution)/shard_map/all_to_all | solution.py:76
  29.9 86.5 %all-to-all-done.1 = bf16[32,2,4,3584]{3,2,1,0:T(4,128)(2,1)S(1)} async-done(((bf16[32,2,4,3584]{3,2,1,0:T(4,128)(2,1)}), bf16[32,2,4,3584]{3,2,1,0:T(4,128)(2,1)S(1)}, u32[]{:S(2)}, u32[]{:S(2)}) %all-to-all-start.1) | async-done | bytes 1835040 | tf_op jit(solution)/shard_map/all_to_all | solution.py:76
  116.4 1.8 broadcast_in_dim.56
  118.2 4.9 all-to-all-start
  124.3 3.1 fusion.21
  127.4 25.3 %all-gather.8.cloned.1.call-done = bf16[3584,256]{1,0:T(8,128)(2,1)} async-done(((bf16[224,256]{1,0:T(8,128)(2,1)}), bf16[3584,256]{1,0:T(8,128)(2,1)}) %all-gather.8.cloned.1.call-update) | async-done | bytes 1835024 | tf_op jit(solution)/shard_map/all_gather | solution.py:114
  152.8 8.4 %broadcast_in_dim.64 = f32[3584,2,128]{2,1,0:T(2,128)S(1)} broadcast(f32[3584,2]{1,0:T(8,128)S(1)} %bitcast.103), dimensions={0,1} | broadcast | bytes 3698688 | tf_op jit(solution)/shard_map/broadcast_in_dim | solution.py:13
  161.6 53.3 %all-gather.6.cloned.1.call-done = bf16[3584,256]{1,0:T(8,128)(2,1)} async-done(((bf16[224,256]{1,0:T(8,128)(2,1)}), bf16[3584,256]{1,0:T(8,128)(2,1)}) %all-gather.6.cloned.1.call-update) | async-done | bytes 1835024 | tf_op jit(solution)/shard_map/all_gather | solution.py:115
  215.1 8.2 %broadcast_in_dim.62 = f32[3584,2,128]{2,1,0:T(2,128)S(1)} broadcast(f32[3584,2]{1,0:T(8,128)S(1)} %bitcast.104), dimensions={0,1} | broadcast | bytes 3698688 | tf_op jit(solution)/shard_map/broadcast_in_dim | solution.py:13
  225.0 1.9 fusion.36
  228.5 2.4 reshape_squeeze.13
  234.4 3.3 fusion.35
  237.7 2.4 reshape_squeeze.14
  240.1 2.4 reshape_squeeze.12
  242.5 2.0 fusion.3
  251.0 29.2 %copy.80 = bf16[3,3584,256]{2,0,1:T(4,128)(2,1)} copy(bf16[3,3584,256]{2,1,0:T(8,128)(2,1)S(1)} %pad_maximum_fusion) | data formatting | bytes 11010048 | tf_op jit(solution)/shard_map/stack | solution.py:149
  280.2 7.2 %all-to-all-start.3 = ((bf16[3,3584,256]{2,0,1:T(4,128)(2,1)}), bf16[3,3584,256]{2,0,1:T(4,128)(2,1)}, u32[]{:S(2)}, u32[]{:S(2)}) async-start(bf16[3,3584,256]{2,0,1:T(4,128)(2,1)} %copy.80), calls=%async_computation.3 | async-start | bytes 14680064 | tf_op jit(solution)/shard_map/all_to_all | solution.py:150
  290.6 1.8 stack_reshape.7
  294.8 2.4 pad_maximum_fusion.1
  297.3 105.3 %all-to-all-done.3 = bf16[3,3584,256]{2,0,1:T(4,128)(2,1)} async-done(((bf16[3,3584,256]{2,0,1:T(4,128)(2,1)}), bf16[3,3584,256]{2,0,1:T(4,128)(2,1)}, u32[]{:S(2)}, u32[]{:S(2)}) %all-to-all-start.3) | async-done | bytes 5505056 | tf_op jit(solution)/shard_map/all_to_all | solution.py:150
  402.6 12.9 %all-to-all-start.2 = ((bf16[32,2,4,3584]{3,2,1,0:T(4,128)(2,1)}), bf16[32,2,4,3584]{3,2,1,0:T(4,128)(2,1)S(1)}, u32[]{:S(2)}, u32[]{:S(2)}) async-start(bf16[32,2,4,3584]{3,2,1,0:T(4,128)(2,1)} %pad_maximum_fusion.1), calls=%async_computation.2 | async-start | bytes 3670016 | tf_op jit(solution)/shard_map/all_to_all | solution.py:140
  415.5 6.4 %reduce_sum.42 = bf16[3,224,256]{2,0,1:T(4,128)(2,1)S(1)} reduce(bf16[3,16,224,256]{3,0,2,1:T(4,128)(2,1)} %bitcast.18, bf16[]{:T(256)} %constant.33.clone.1), dimensions={1}, to_apply=%region_5.6 | reduce | flops 2580480 | bytes 5849090 | tf_op jit(solution)/shard_map/reduce_sum | solution.py:152
  424.4 80.0 %all-to-all-done.2 = bf16[32,2,4,3584]{3,2,1,0:T(4,128)(2,1)S(1)} async-done(((bf16[32,2,4,3584]{3,2,1,0:T(4,128)(2,1)}), bf16[32,2,4,3584]{3,2,1,0:T(4,128)(2,1)S(1)}, u32[]{:S(2)}, u32[]{:S(2)}) %all-to-all-start.2) | async-done | bytes 1835040 | tf_op jit(solution)/shard_map/all_to_all | solution.py:140
  505.2 1.9 fusion.15
  (102 shorter events, 30.2 us)
Async XLA Ops:
  7.2 2.8 copy-start
  12.1 17.1 %copy-start.15 = (s32[128,8]{0,1:T(8,128)S(1)}, s32[128,8]{0,1:T(8,128)}, u32[]{:S(2)}) copy-start(s32[128,8]{0,1:T(8,128)} %param.15) | copy-start | bytes 12292
  12.1 17.1 %copy-start.16 = (f32[128,8]{0,1:T(8,128)S(1)}, f32[128,8]{0,1:T(8,128)}, u32[]{:S(2)}) copy-start(f32[128,8]{0,1:T(8,128)} %param.14) | copy-start | bytes 12292
  12.1 17.3 %copy-start.14 = (bf16[128,3584]{1,0:T(8,128)(2,1)S(1)}, bf16[128,3584]{1,0:T(8,128)(2,1)}, u32[]{:S(2)}) copy-start(bf16[128,3584]{1,0:T(8,128)(2,1)} %param.13) | copy-start | bytes 2752516
  12.1 104.2 %all-to-all-start.1 = ((bf16[32,2,4,3584]{3,2,1,0:T(4,128)(2,1)}), bf16[32,2,4,3584]{3,2,1,0:T(4,128)(2,1)S(1)}, u32[]{:S(2)}, u32[]{:S(2)}) async-start(bf16[32,2,4,3584]{3,2,1,0:T(4,128)(2,1)} %bitcast.102), calls=%async_computation.1 | async-start | bytes 3670016 | tf_op jit(solution)/shard_map/all_to_all | solution.py:76
  27.8 96.5 %all-gather.4.cloned.1.call-start = ((), (), s32[]{:S(2)}) async-start(), calls=%async_computation.4 | async-start | bytes 1949696 | tf_op jit(solution)/shard_map/all_gather | solution.py:116
  28.5 124.2 %all-gather.8.cloned.1.call-start = ((), (), s32[]{:S(2)}) async-start(), calls=%async_computation.6 | async-start | bytes 1949696 | tf_op jit(solution)/shard_map/all_gather | solution.py:114
  116.4 1.8 copy-start.7
  118.2 5.6 %copy-start.17 = (f32[28,2]{0,1:T(2,128)S(1)}, f32[28,2]{0,1:T(2,128)}, u32[]{:S(2)}) copy-start(f32[28,2]{0,1:T(2,128)} %param.21) | copy-start | bytes 676
  118.2 5.7 %copy-start.18 = (f32[28,2]{0,1:T(2,128)S(1)}, f32[28,2]{0,1:T(2,128)}, u32[]{:S(2)}) copy-start(f32[28,2]{0,1:T(2,128)} %param.22) | copy-start | bytes 676
  118.2 5.8 %copy-start.19 = (f32[2,28]{1,0:T(2,128)S(1)}, f32[2,28]{1,0:T(2,128)}, u32[]{:S(2)}) copy-start(f32[2,28]{1,0:T(2,128)} %param.23) | copy-start | bytes 676
  118.2 116.2 %all-to-all-start = ((bf16[32,2,4,3584]{3,2,1,0:T(4,128)(2,1)}), bf16[32,2,4,3584]{3,2,1,0:T(4,128)(2,1)}, u32[]{:S(2)}, u32[]{:S(2)}) async-start(bf16[32,2,4,3584]{3,2,1,0:T(4,128)(2,1)} %bitcast.101), calls=%async_computation | async-start | bytes 3670016 | tf_op jit(solution)/shard_map/all_to_all | solution.py:79
  123.1 91.9 %all-gather.6.cloned.1.call-start = ((), (), s32[]{:S(2)}) async-start(), calls=%async_computation.5 | async-start | bytes 1949696 | tf_op jit(solution)/shard_map/all_gather | solution.py:115
  152.8 8.4 %copy-start.11 = (bf16[3584,256]{1,0:T(8,128)(2,1)S(1)}, bf16[3584,256]{1,0:T(8,128)(2,1)}, u32[]{:S(2)}) copy-start(bf16[3584,256]{1,0:T(8,128)(2,1)} %all-gather.8.cloned.1.call-done) | copy-start | bytes 5505028
  215.1 8.2 %copy-start.12 = (bf16[3584,256]{1,0:T(8,128)(2,1)S(1)}, bf16[3584,256]{1,0:T(8,128)(2,1)}, u32[]{:S(2)}) copy-start(bf16[3584,256]{1,0:T(8,128)(2,1)} %all-gather.6.cloned.1.call-done) | copy-start | bytes 5505028
  223.3 1.7 copy-start.8
  230.9 1.5 copy-start.2
  242.5 2.0 copy-start.10
  242.5 2.1 copy-start.13
  280.2 122.4 %all-to-all-start.3 = ((bf16[3,3584,256]{2,0,1:T(4,128)(2,1)}), bf16[3,3584,256]{2,0,1:T(4,128)(2,1)}, u32[]{:S(2)}, u32[]{:S(2)}) async-start(bf16[3,3584,256]{2,0,1:T(4,128)(2,1)} %copy.80), calls=%async_computation.3 | async-start | bytes 14680064 | tf_op jit(solution)/shard_map/all_to_all | solution.py:150
  287.4 1.5 copy-start.3
  292.4 1.5 copy-start.4
  402.6 101.8 %all-to-all-start.2 = ((bf16[32,2,4,3584]{3,2,1,0:T(4,128)(2,1)}), bf16[32,2,4,3584]{3,2,1,0:T(4,128)(2,1)S(1)}, u32[]{:S(2)}, u32[]{:S(2)}) async-start(bf16[32,2,4,3584]{3,2,1,0:T(4,128)(2,1)} %pad_maximum_fusion.1), calls=%async_computation.2 | async-start | bytes 3670016 | tf_op jit(solution)/shard_map/all_to_all | solution.py:140
  504.4 2.7 copy-start.1
  (3 other events, 3.5 us)
Sparse Core Ops, SparseCore 0:
  31.6 58.7 all-gather.3
  93.5 59.1 all-gather.7
  155.7 59.1 all-gather.5
where the time goes:
time: 515 us; the launch traced here: 514 us
  waiting for transfers between devices  353 us (69%)
  local copies, waits for them, and re-layouts  73.9 us (14%)
  starting transfers between devices  40.7 us (8%)
  other arithmetic  17.5 us (3%)
  between operations  14.8 us (3%)
  matrix products  14.2 us (3%)
    all_to_all x1, waiting for transfers between devices, on_device(): lax.all_to_all(stacked, 'dp', split_axis=1, concat_axis=0, tiled=True)  105 us
    all_to_all x1, waiting for transfers between devices, send_rows(): lax.all_to_all(fan_out(token_rows, members), 'expert', split_axis=0, conc...  86.5 us
    all_to_all x1, waiting for transfers between devices, on_device(): lax.all_to_all(dx_parts, 'expert', split_axis=0, concat_axis=0, tiled=True)  80 us
    all_gather x1, waiting for transfers between devices, on_device(): lax.all_gather(w_up, 'dp', axis=0, tiled=True)  53.3 us
    another operation x1, local copies, waits for them, and re-layouts, on_device(): stacked = jnp.stack([sum_gate, sum_up, sum_down], axis=0)  29.2 us
    all_gather x1, waiting for transfers between devices, on_device(): lax.all_gather(w_gate, 'dp', axis=0, tiled=True)  25.3 us
    broadcast_in_dim x2, local copies, waits for them, and re-layouts, dequantize(): jnp.repeat(jnp.repeat(scale, block_rows, axis=0), block_cols, axis=1)  16.6 us
    all_to_all x1, starting transfers between devices, send_rows(): lax.all_to_all(fan_out(token_rows, members), 'expert', split_axis=0, conc...  15.6 us
  transfers between devices with their start and end apart: 7, of which 5 were waited for; matrix products, arithmetic and copies ran while one was open for 10% of the time, Pallas kernels for 0%

commit v1 on v0

--- a/solution.py
+++ b/solution.py
@@ -112,7 +112,9 @@
     )
     gathered = (
         lax.all_gather(w_gate, "dp", axis=0, tiled=True),
-        lax.all_gather(w_up, "dp", axis=0, tiled=True),
+        jnp.concatenate(
+            lax.all_to_all(jnp.stack([w_up] * lax.axis_size("dp")), "dp", 0, 0), axis=0
+        ),
         lax.all_gather(w_down, "dp", axis=1, tiled=True),
     )
     full_gate, full_up, full_down = gathered

time: 515 us -> 531 us (1.031)
  starting transfers between devices: 40.7 us -> 55.3 us
  waiting for transfers between devices: 353 us -> 339 us
  other arithmetic: 17.5 us -> 24.6 us
  local copies, waits for them, and re-layouts: 73.9 us -> 80.9 us
    all_gather x1 -> x0, waiting for transfers between devices: 53.3 us -> none  [on_device(): lax.all_gather(w_up, 'dp', axis=0, tiled=True)]
    all_to_all x0 -> x1, waiting for transfers between devices: none -> 19.8 us  [on_device(): lax.all_to_all(jnp.stack([w_up] * lax.axis_size('dp')), 'dp', 0, 0)]
    all_gather x1, waiting for transfers between devices: 25.3 us -> 43.4 us  [on_device(): lax.all_gather(w_gate, 'dp', axis=0, tiled=True)]
    all_to_all x1, waiting for transfers between devices: 0.01 us -> 9.45 us  [send_rows(): lax.all_to_all(fan_out(cot_rows, members), 'expert', split_axis=0, concat...]
    all_to_all x0 -> x1, starting transfers between devices: none -> 9.32 us  [on_device(): lax.all_to_all(jnp.stack([w_up] * lax.axis_size('dp')), 'dp', 0, 0)]
    convert_element_type x3 -> x4, other arithmetic: 5.2 us -> 13.9 us  [dequantize(): return (values.astype(jnp.float32) * spread).astype(jnp.bfloat16)]
    all_to_all x1, waiting for transfers between devices: 105 us -> 98.4 us  [on_device(): lax.all_to_all(stacked, 'dp', split_axis=1, concat_axis=0, tiled=True)]
  transfers between devices with their start and end apart: 7 -> 7, of which waited for: 5 -> 6; matrix products, arithmetic and copies ran while one was open for 10% -> 12% of each run, Pallas kernels for 0% -> 0%
where the time goes in v1:
time: 531 us; the launch traced here: 529 us
  waiting for transfers between devices  339 us (64%)
  local copies, waits for them, and re-layouts  80.9 us (15%)
  starting transfers between devices  55.3 us (10%)
  other arithmetic  24.6 us (5%)
  between operations  15.1 us (3%)
  matrix products  14.2 us (3%)
    all_to_all x1, waiting for transfers between devices, on_device(): lax.all_to_all(stacked, 'dp', split_axis=1, concat_axis=0, tiled=True)  98.4 us
    all_to_all x1, waiting for transfers between devices, send_rows(): lax.all_to_all(fan_out(token_rows, members), 'expert', split_axis=0, conc...  87.3 us
    all_to_all x1, waiting for transfers between devices, on_device(): lax.all_to_all(dx_parts, 'expert', split_axis=0, concat_axis=0, tiled=True)  79.8 us
    all_gather x1, waiting for transfers between devices, on_device(): lax.all_gather(w_gate, 'dp', axis=0, tiled=True)  43.4 us
    another operation x1, local copies, waits for them, and re-layouts, on_device(): stacked = jnp.stack([sum_gate, sum_up, sum_down], axis=0)  29.3 us
    all_to_all x1, waiting for transfers between devices, on_device(): lax.all_to_all(jnp.stack([w_up] * lax.axis_size('dp')), 'dp', 0, 0)  19.8 us
    all_to_all x1, starting transfers between devices, on_device(): lax.all_to_all(dx_parts, 'expert', split_axis=0, concat_axis=0, tiled=True)  17 us
    broadcast_in_dim x2, local copies, waits for them, and re-layouts, dequantize(): jnp.repeat(jnp.repeat(scale, block_rows, axis=0), block_cols, axis=1)  16.6 us
  transfers between devices with their start and end apart: 7, of which 6 were waited for; matrix products, arithmetic and copies ran while one was open for 12% of the time, Pallas kernels for 0%

profile of v1, /device:TPU:20, one launch (start us, length us, event | category | flops | bytes accessed | tf_op | source)
XLA Modules:
  0.0 529.4 jit_solution(14580718175447703445)
XLA Ops:
  7.2 2.4 stack.15
  9.6 9.3 %all-to-all-start.2 = ((bf16[16,224,256]{2,1,0:T(8,128)(2,1)}), bf16[16,224,256]{2,1,0:T(8,128)(2,1)S(1)}, u32[]{:S(2)}, u32[]{:S(2)}) async-start(bf16[16,224,256]{2,1,0:T(8,128)(2,1)} %stack.15), calls=%async_computation.2 | async-start | bytes 3670016 | tf_op jit(solution)/shard_map/all_to_all | solution.py:116
  20.7 19.8 %all-to-all-done.2 = bf16[16,224,256]{2,1,0:T(8,128)(2,1)S(1)} async-done(((bf16[16,224,256]{2,1,0:T(8,128)(2,1)}), bf16[16,224,256]{2,1,0:T(8,128)(2,1)S(1)}, u32[]{:S(2)}, u32[]{:S(2)}) %all-to-all-start.2) | async-done | bytes 1835040 | tf_op jit(solution)/shard_map/all_to_all | solution.py:116
  42.3 15.9 %all-to-all-start.1 = ((bf16[32,2,4,3584]{3,2,1,0:T(4,128)(2,1)}), bf16[32,2,4,3584]{3,2,1,0:T(4,128)(2,1)}, u32[]{:S(2)}, u32[]{:S(2)}) async-start(bf16[32,2,4,3584]{3,2,1,0:T(4,128)(2,1)} %bitcast.109), calls=%async_computation.1 | async-start | bytes 3670016 | tf_op jit(solution)/shard_map/all_to_all | solution.py:76
  59.6 87.3 %all-to-all-done.1 = bf16[32,2,4,3584]{3,2,1,0:T(4,128)(2,1)} async-done(((bf16[32,2,4,3584]{3,2,1,0:T(4,128)(2,1)}), bf16[32,2,4,3584]{3,2,1,0:T(4,128)(2,1)}, u32[]{:S(2)}, u32[]{:S(2)}) %all-to-all-start.1) | async-done | bytes 1835040 | tf_op jit(solution)/shard_map/all_to_all | solution.py:76
  148.7 4.9 all-to-all-start
  156.7 3.0 reshape.373
  159.7 9.9 %multiply_convert_fusion = bf16[3584,2,128]{2,1,0:T(2,128)(2,1)} fusion(f32[3584,2,128]{2,1,0:T(2,128)} %reshape.373, f32[3584,2]{1,0:T(8,128)} %copy.86), kind=kLoop, calls=%fused_computation.38 | loop fusion | flops 1835008 | bytes 5533696 | tf_op jit(solution)/shard_map/convert_element_type | solution.py:14
  169.7 3.1 fusion.21
  172.8 43.4 %all-gather.5.cloned.1.call-done = bf16[3584,256]{1,0:T(8,128)(2,1)} async-done(((bf16[224,256]{1,0:T(8,128)(2,1)}), bf16[3584,256]{1,0:T(8,128)(2,1)}) %all-gather.5.cloned.1.call-update) | async-done | bytes 1835024 | tf_op jit(solution)/shard_map/all_gather | solution.py:114
  216.3 8.2 %broadcast_in_dim.64 = f32[3584,2,128]{2,1,0:T(2,128)S(1)} broadcast(f32[3584,2]{1,0:T(8,128)S(1)} %bitcast.110), dimensions={0,1} | broadcast | bytes 3698688 | tf_op jit(solution)/shard_map/broadcast_in_dim | solution.py:13
  224.9 3.0 fusion.42
  234.3 9.5 %all-to-all-done = bf16[32,2,4,3584]{3,2,1,0:T(4,128)(2,1)} async-done(((bf16[32,2,4,3584]{3,2,1,0:T(4,128)(2,1)}), bf16[32,2,4,3584]{3,2,1,0:T(4,128)(2,1)}, u32[]{:S(2)}, u32[]{:S(2)}) %all-to-all-start) | async-done | bytes 1835040 | tf_op jit(solution)/shard_map/all_to_all | solution.py:79
  243.7 3.3 fusion.41
  247.1 2.4 reshape_squeeze.12
  249.4 2.4 reshape_squeeze.14
  260.0 29.3 %copy.92 = bf16[3,3584,256]{2,0,1:T(4,128)(2,1)} copy(bf16[3,3584,256]{2,1,0:T(8,128)(2,1)S(1)} %pad_maximum_fusion) | data formatting | bytes 11010048 | tf_op jit(solution)/shard_map/stack | solution.py:151
  289.3 8.1 %all-to-all-start.4 = ((bf16[3,3584,256]{2,0,1:T(4,128)(2,1)}), bf16[3,3584,256]{2,0,1:T(4,128)(2,1)}, u32[]{:S(2)}, u32[]{:S(2)}) async-start(bf16[3,3584,256]{2,0,1:T(4,128)(2,1)} %copy.92), calls=%async_computation.4 | async-start | bytes 14680064 | tf_op jit(solution)/shard_map/all_to_all | solution.py:152
  297.4 8.4 %broadcast_in_dim.62 = f32[3584,2,128]{2,1,0:T(2,128)S(1)} broadcast(f32[3584,2]{1,0:T(8,128)} %copy.86), dimensions={0,1} | broadcast | bytes 3698688 | tf_op jit(solution)/shard_map/broadcast_in_dim | solution.py:13
  313.4 2.4 pad_maximum_fusion.1
  315.8 98.4 %all-to-all-done.4 = bf16[3,3584,256]{2,0,1:T(4,128)(2,1)} async-done(((bf16[3,3584,256]{2,0,1:T(4,128)(2,1)}), bf16[3,3584,256]{2,0,1:T(4,128)(2,1)}, u32[]{:S(2)}, u32[]{:S(2)}) %all-to-all-start.4) | async-done | bytes 5505056 | tf_op jit(solution)/shard_map/all_to_all | solution.py:152
  414.2 17.0 %all-to-all-start.3 = ((bf16[32,2,4,3584]{3,2,1,0:T(4,128)(2,1)}), bf16[32,2,4,3584]{3,2,1,0:T(4,128)(2,1)S(1)}, u32[]{:S(2)}, u32[]{:S(2)}) async-start(bf16[32,2,4,3584]{3,2,1,0:T(4,128)(2,1)} %pad_maximum_fusion.1), calls=%async_computation.3 | async-start | bytes 3670016 | tf_op jit(solution)/shard_map/all_to_all | solution.py:142
  431.2 6.4 %reduce_sum.42 = bf16[3,224,256]{2,0,1:T(4,128)(2,1)S(1)} reduce(bf16[3,16,224,256]{3,0,2,1:T(4,128)(2,1)} %bitcast.19, bf16[]{:T(256)} %constant.33.clone.1), dimensions={1}, to_apply=%region_5.6 | reduce | flops 2580480 | bytes 5849090 | tf_op jit(solution)/shard_map/reduce_sum | solution.py:154
  440.0 79.8 %all-to-all-done.3 = bf16[32,2,4,3584]{3,2,1,0:T(4,128)(2,1)S(1)} async-done(((bf16[32,2,4,3584]{3,2,1,0:T(4,128)(2,1)}), bf16[32,2,4,3584]{3,2,1,0:T(4,128)(2,1)S(1)}, u32[]{:S(2)}, u32[]{:S(2)}) %all-to-all-start.3) | async-done | bytes 1835040 | tf_op jit(solution)/shard_map/all_to_all | solution.py:142
  (105 shorter events, 36.9 us)
Async XLA Ops:
  7.2 13.1 %copy-start = (bf16[128,3584]{1,0:T(8,128)(2,1)S(1)}, bf16[128,3584]{1,0:T(8,128)(2,1)}, u32[]{:S(2)}) copy-start(bf16[128,3584]{1,0:T(8,128)(2,1)} %param.12) | copy-start | bytes 2752516
  9.6 10.1 %copy-start.14 = (s32[128,8]{0,1:T(8,128)S(1)}, s32[128,8]{0,1:T(8,128)}, u32[]{:S(2)}) copy-start(s32[128,8]{0,1:T(8,128)} %param.15) | copy-start | bytes 12292
  9.6 10.1 %copy-start.19 = (s32[1,4]{1,0:T(1,128)S(1)}, s32[1,4]{1,0:T(1,128)}, u32[]{:S(2)}) copy-start(s32[1,4]{1,0:T(1,128)} %param.17) | copy-start | bytes 52
  9.6 30.8 %all-to-all-start.2 = ((bf16[16,224,256]{2,1,0:T(8,128)(2,1)}), bf16[16,224,256]{2,1,0:T(8,128)(2,1)S(1)}, u32[]{:S(2)}, u32[]{:S(2)}) async-start(bf16[16,224,256]{2,1,0:T(8,128)(2,1)} %stack.15), calls=%async_computation.2 | async-start | bytes 3670016 | tf_op jit(solution)/shard_map/all_to_all | solution.py:116
  40.4 116.3 %copy-start.4 = (bf16[16,224,256]{2,1,0:T(8,128)(2,1)}, bf16[16,224,256]{2,1,0:T(8,128)(2,1)S(1)}, u32[]{:S(2)}) copy-start(bf16[16,224,256]{2,1,0:T(8,128)(2,1)S(1)} %all-to-all-done.2) | copy-start | bytes 5505028
  42.3 16.6 %copy-start.15 = (f32[128,8]{0,1:T(8,128)S(1)}, f32[128,8]{0,1:T(8,128)}, u32[]{:S(2)}) copy-start(f32[128,8]{0,1:T(8,128)} %param.14) | copy-start | bytes 12292
  42.3 16.8 %copy-start.13 = (bf16[128,3584]{1,0:T(8,128)(2,1)S(1)}, bf16[128,3584]{1,0:T(8,128)(2,1)}, u32[]{:S(2)}) copy-start(bf16[128,3584]{1,0:T(8,128)(2,1)} %param.13) | copy-start | bytes 2752516
  42.3 104.5 %all-to-all-start.1 = ((bf16[32,2,4,3584]{3,2,1,0:T(4,128)(2,1)}), bf16[32,2,4,3584]{3,2,1,0:T(4,128)(2,1)}, u32[]{:S(2)}, u32[]{:S(2)}) async-start(bf16[32,2,4,3584]{3,2,1,0:T(4,128)(2,1)} %bitcast.109), calls=%async_computation.1 | async-start | bytes 3670016 | tf_op jit(solution)/shard_map/all_to_all | solution.py:76
  58.2 111.4 %all-gather.3.cloned.1.call-start = ((), (), s32[]{:S(2)}) async-start(), calls=%async_computation.5 | async-start | bytes 1949696 | tf_op jit(solution)/shard_map/all_gather | solution.py:118
  148.7 5.6 %copy-start.16 = (f32[28,2]{0,1:T(2,128)S(1)}, f32[28,2]{0,1:T(2,128)}, u32[]{:S(2)}) copy-start(f32[28,2]{0,1:T(2,128)} %param.21) | copy-start | bytes 676
  148.7 5.7 %copy-start.17 = (f32[28,2]{0,1:T(2,128)S(1)}, f32[28,2]{0,1:T(2,128)}, u32[]{:S(2)}) copy-start(f32[28,2]{0,1:T(2,128)} %param.22) | copy-start | bytes 676
  148.7 5.8 %copy-start.18 = (f32[2,28]{1,0:T(2,128)S(1)}, f32[2,28]{1,0:T(2,128)}, u32[]{:S(2)}) copy-start(f32[2,28]{1,0:T(2,128)} %param.23) | copy-start | bytes 676
  148.7 95.1 %all-to-all-start = ((bf16[32,2,4,3584]{3,2,1,0:T(4,128)(2,1)}), bf16[32,2,4,3584]{3,2,1,0:T(4,128)(2,1)}, u32[]{:S(2)}, u32[]{:S(2)}) async-start(bf16[32,2,4,3584]{3,2,1,0:T(4,128)(2,1)} %bitcast.108), calls=%async_computation | async-start | bytes 3670016 | tf_op jit(solution)/shard_map/all_to_all | solution.py:79
  153.6 62.6 %all-gather.5.cloned.1.call-start = ((), (), s32[]{:S(2)}) async-start(), calls=%async_computation.6 | async-start | bytes 1949696 | tf_op jit(solution)/shard_map/all_gather | solution.py:114
  216.3 8.2 %copy-start.10 = (bf16[3584,256]{1,0:T(8,128)(2,1)S(1)}, bf16[3584,256]{1,0:T(8,128)(2,1)}, u32[]{:S(2)}) copy-start(bf16[3584,256]{1,0:T(8,128)(2,1)} %all-gather.5.cloned.1.call-done) | copy-start | bytes 5505028
  232.0 1.5 copy-start.11
  251.8 2.0 copy-start.9
  251.8 2.1 copy-start.12
  289.3 124.9 %all-to-all-start.4 = ((bf16[3,3584,256]{2,0,1:T(4,128)(2,1)}), bf16[3,3584,256]{2,0,1:T(4,128)(2,1)}, u32[]{:S(2)}, u32[]{:S(2)}) async-start(bf16[3,3584,256]{2,0,1:T(4,128)(2,1)} %copy.92), calls=%async_computation.4 | async-start | bytes 14680064 | tf_op jit(solution)/shard_map/all_to_all | solution.py:152
  297.4 8.4 %copy-start.5 = (bf16[16,224,256]{2,1,0:T(8,128)(2,1)S(1)}, bf16[16,224,256]{2,1,0:T(8,128)(2,1)}, u32[]{:S(2)}) copy-start(bf16[16,224,256]{2,1,0:T(8,128)(2,1)} %copy-done.4) | copy-start | bytes 5505028
  306.2 1.2 copy-start.2
  310.9 1.5 copy-start.3
  414.2 105.6 %all-to-all-start.3 = ((bf16[32,2,4,3584]{3,2,1,0:T(4,128)(2,1)}), bf16[32,2,4,3584]{3,2,1,0:T(4,128)(2,1)S(1)}, u32[]{:S(2)}, u32[]{:S(2)}) async-start(bf16[32,2,4,3584]{3,2,1,0:T(4,128)(2,1)} %pad_maximum_fusion.1), calls=%async_computation.3 | async-start | bytes 3670016 | tf_op jit(solution)/shard_map/all_to_all | solution.py:142
  519.8 2.7 copy-start.1
  (3 other events, 3.5 us)
Sparse Core Ops, SparseCore 0:
  62.1 58.6 all-gather.2
  157.4 58.6 all-gather.4
